TPU v7x, 512 devices: a whole 4x4x16 slice. The times are simulated.
512 devices in a mesh: ia: 64 (over x, z_lo, core), jb: 8 (over y, z_hi).
Axes of the slice: x: 4, y: 4, z: 16 (z_hi: 2, z_lo: 8; z = z_hi * 8 + z_lo), core: 2. Of those that a mesh axis runs over, the one named last changes fastest.
Arguments:
- density: bfloat16 [8000, 100000], P('ia', 'jb'), may hold values from -6 to 6
- chol_vectors: bfloat16 [100000, 512], P('jb', 'ia'), may hold values from -0.01953125 to 0.01953125
- virt_coef: bfloat16 [1000, 1100], P('jb'), may hold values from -0.1875 to 0.1875
Outputs:
- half_back: float32 [8, 512, 1100], P(None, ('ia', 'jb'))
All inputs are finite; a program needn't handle non-finite values.
Results may differ from a plain program's by a relative error of at most 0.0003.
Values may be sent and summed in bfloat16 or wider, within the bound.
No kernel may reach another device: no remote copies, remote signals or barrier semaphores. Data moves between devices by JAX's collectives and lax.ppermute only.
A program may use at most 64 MiB of HBM per device.

v0:
```python
import jax
import jax.numpy as jnp
from jax import lax
from jax.sharding import Mesh
from jax.sharding import PartitionSpec as P

JB = ("jb_0", "jb_1")
IA_JB = ("ia", "jb_0", "jb_1")


def from_root(shard, axis, root):
    return lax.dynamic_index_in_dim(lax.all_gather(shard, axis), root, 0, keepdims=False)


def summed_rows(shard, axes, dim):
    for axis in axes:
        shard = lax.psum_scatter(shard, axis, scatter_dimension=dim, tiled=True)
    return shard


def on_device(density, chol_vectors, virt_coef):
    row_count = density.shape[0]
    groups = lax.axis_size(JB)
    slab_devices = lax.axis_size("ia")
    all_vectors = lax.all_gather(chol_vectors, "ia", axis=1, tiled=True)
    gamma_part = jnp.dot(density, all_vectors, preferred_element_type=jnp.float32)
    owner_row = lax.axis_index("ia") % groups
    coef_block = from_root(virt_coef, JB, owner_row).astype(jnp.float32)
    chol_count = gamma_part.shape[1]
    group_width = chol_count // slab_devices
    reduced = summed_rows(gamma_part.reshape(row_count, slab_devices, group_width), JB, 2)
    summed = jnp.einsum("arq,an->rqn", reduced, coef_block, precision=lax.Precision.HIGHEST)
    regrouped = lax.all_to_all(summed, "ia", split_axis=0, concat_axis=0, tiled=True)
    occ_slab = slab_devices // groups
    return jnp.sum(
        regrouped.reshape(occ_slab, groups, regrouped.shape[1], regrouped.shape[2]), axis=1
    )


def solution(mesh):
    split = Mesh(mesh.devices.reshape(mesh.shape["ia"], 4, 2), ("ia", "jb_0", "jb_1"))
    return jax.shard_map(
        on_device,
        mesh=split,
        in_specs=(P("ia", JB), P(JB, "ia"), P(JB, None)),
        out_specs=P(None, IA_JB, None),
        check_vma=False,
    )
```

profile of v0, /device:TPU:1, one launch (start us, length us, event | category | flops | bytes accessed | tf_op | source)
XLA Modules:
  0.0 315.7 jit_solution(6847420634601952481)
XLA Ops:
  7.4 0.0 copy-start
  7.4 0.0 all-gather.5.cloned.1.call-start
  7.4 0.7 all-gather.5.cloned.1.call-update
  8.1 0.0 reduce-scatter.3.cloned.1.call-start
  8.1 140.4 %all-gather.5.cloned.1.call-done = bf16[12500,512]{0,1:T(8,128)(2,1)} async-done(((bf16[12500,8]{0,1:T(8,128)(2,1)}), bf16[12500,512]{0,1:T(8,128)(2,1)}) %all-gather.5.cloned.1.call-update) | async-done | bytes 12800016 | tf_op jit(solution)/shard_map/all_gather | solution.py:25
  148.5 0.0 copy-done
  148.5 6.5 %convolution_bitcast_fusion.1 = f32[125,64,8]{0,2,1:T(8,128)S(1)} fusion(bf16[125,12500]{0,1:T(8,128)(2,1)S(1)} %copy-done, bf16[12500,512]{0,1:T(8,128)(2,1)} %all-gather.5.cloned.1.call-done), kind=kOutput, calls=%fused_computation.1 | convolution fusion | flops 1600000000 | bytes 16181000 | tf_op jit(solution)/shard_map/dot_general | solution.py:26
  155.1 0.8 copy.6
  155.8 0.0 reduce-scatter.3.cloned.1.call-update
  155.8 0.0 all-gather.7.cloned.1.call-start
  155.9 0.5 all-gather.7.cloned.1.call-update
  156.4 0.0 reduce-scatter.5.cloned.1.call-start
  156.5 21.4 %reduce-scatter.3.cloned.1.call-done = f32[125,64,2]{0,1,2:T(8,128)} async-done(((f32[125,64,8]{0,1,2:T(8,128)}), f32[125,64,2]{0,1,2:T(8,128)}) %reduce-scatter.3.cloned.1.call-update) | async-done | bytes 64016 | tf_op jit(solution)/shard_map/reduce_scatter | solution.py:17
  177.9 0.0 reduce-scatter.5.cloned.1.call-update
  178.0 98.3 %all-gather.7.cloned.1.call-done = bf16[8,125,1100]{1,2,0:T(8,128)(2,1)} async-done(((bf16[1,125,1100]{1,2,0:T(8,128)(2,1)}), bf16[8,125,1100]{1,2,0:T(8,128)(2,1)}) %all-gather.7.cloned.1.call-update) | async-done | bytes 2200016 | tf_op jit(solution)/shard_map/all_gather | solution.py:12
  276.3 0.0 reduce-scatter.5.cloned.1.call-done
  276.3 1.4 convolution_bitcast_fusion
  277.7 0.3 copy.7
  278.0 29.9 %all_to_all.5 = f32[64,1,1100]{2,1,0:T(1,128)S(1)} all-to-all(f32[64,1,1100]{2,1,0:T(1,128)S(1)} %copy.7), channel_id=1, replica_groups=mesh['ia'=64,'jb_0'=4,'jb_1'=2] {'ia'}, dimensions={0} | all-to-all | bytes 563200 | tf_op jit(solution)/shard_map/all_to_all | solution.py:33
  307.9 0.1 bitcast_reduce_fusion
  308.0 0.6 reduce_sum.12
Async XLA Ops:
  7.4 141.2 %copy-start = (bf16[125,12500]{0,1:T(8,128)(2,1)S(1)}, bf16[125,12500]{0,1:T(8,128)(2,1)}, u32[]{:S(2)}) copy-start(bf16[125,12500]{0,1:T(8,128)(2,1)} %param.3) | copy-start | bytes 9375004
  7.4 141.2 %all-gather.5.cloned.1.call-start = ((), (), s32[]{:S(2)}) async-start(), calls=%async_computation.3 | async-start | bytes 13045760 | tf_op jit(solution)/shard_map/all_gather | solution.py:25
  8.1 169.8 %reduce-scatter.3.cloned.1.call-start = ((), (), s32[]{:S(2)}) async-start(), calls=%async_computation.4 | async-start | bytes 327680 | tf_op jit(solution)/shard_map/reduce_scatter | solution.py:17
  155.8 120.4 %all-gather.7.cloned.1.call-start = ((), (), s32[]{:S(2)}) async-start(), calls=%async_computation.6 | async-start | bytes 2543616 | tf_op jit(solution)/shard_map/all_gather | solution.py:12
  156.4 119.9 %reduce-scatter.5.cloned.1.call-start = ((), (), s32[]{:S(2)}) async-start(), calls=%async_computation.5 | async-start | bytes 98304 | tf_op jit(solution)/shard_map/reduce_scatter | solution.py:17
Sparse Core Ops, SparseCore 0:
  10.3 138.1 all-gather.4
  156.0 21.9 reduce-scatter.2
  180.7 33.1 reduce-scatter.4
Sparse Core Ops, SparseCore 1:
  159.5 116.7 all-gather.6
where the time goes:
time: 316 us
  waiting for transfers between devices  261 us (83%)
  blocking collectives  29.9 us (9%)
  between operations  14.6 us (5%)
  matrix products  7.89 us (2%)
    all_gather x1, waiting for transfers between devices, on_device(): all_vectors = lax.all_gather(chol_vectors, 'ia', axis=1, tiled=True)  140 us
    all_gather x1, waiting for transfers between devices, from_root(): lax.all_gather(shard, axis)  98.3 us
    all_to_all x1, blocking collectives, on_device(): lax.all_to_all(summed, 'ia', split_axis=0, concat_axis=0, tiled=True)  29.9 us
    reduce_scatter x2, waiting for transfers between devices, summed_rows(): shard = lax.psum_scatter(shard, axis, scatter_dimension=dim, tiled=True)  21.4 us
    dot_general x1, matrix products, on_device(): jnp.dot(density, all_vectors, preferred_element_type=jnp.float32)  6.51 us
  transfers between devices with their start and end apart: 4, of which 3 were waited for; matrix products, arithmetic and copies ran while one was open for 0% of the time, Pallas kernels for 0%

commit v1 on v0

--- a/solution.py
+++ b/solution.py
@@ -22,7 +22,9 @@
     row_count = density.shape[0]
     groups = lax.axis_size(JB)
     slab_devices = lax.axis_size("ia")
-    all_vectors = lax.all_gather(chol_vectors, "ia", axis=1, tiled=True)
+    all_vectors = jnp.concatenate(
+        lax.all_to_all(jnp.stack([chol_vectors] * lax.axis_size("ia")), "ia", 0, 0), axis=1
+    )
     gamma_part = jnp.dot(density, all_vectors, preferred_element_type=jnp.float32)
     owner_row = lax.axis_index("ia") % groups
     coef_block = from_root(virt_coef, JB, owner_row).astype(jnp.float32)

time: 316 us -> 759 us (2.40)
  blocking collectives: 29.9 us -> 605 us
  waiting for transfers between devices: 261 us -> 120 us
    all_to_all x0 -> x1, blocking collectives: none -> 575 us  [on_device(): lax.all_to_all(jnp.stack([chol_vectors] * lax.axis_size('ia')), 'ia', 0, 0)]
    all_gather x1 -> x0, waiting for transfers between devices: 140 us -> none  [on_device(): all_vectors = lax.all_gather(chol_vectors, 'ia', axis=1, tiled=True)]
  transfers between devices with their start and end apart: 4 -> 3, of which waited for: 3 -> 2; matrix products, arithmetic and copies ran while one was open for 0% -> 0% of each run, Pallas kernels for 0% -> 0%
where the time goes in v1:
time: 759 us
  blocking collectives  605 us (80%)
  waiting for transfers between devices  120 us (16%)
  between operations  14.9 us (2%)
  matrix products  10.3 us (1%)
    all_to_all x1, blocking collectives, on_device(): lax.all_to_all(jnp.stack([chol_vectors] * lax.axis_size('ia')), 'ia', 0, 0)  575 us
    all_gather x1, waiting for transfers between devices, from_root(): lax.all_gather(shard, axis)  98.3 us
    all_to_all x1, blocking collectives, on_device(): lax.all_to_all(summed, 'ia', split_axis=0, concat_axis=0, tiled=True)  29.9 us
    reduce_scatter x2, waiting for transfers between devices, summed_rows(): shard = lax.psum_scatter(shard, axis, scatter_dimension=dim, tiled=True)  21.5 us
  transfers between devices with their start and end apart: 3, of which 2 were waited for; matrix products, arithmetic and copies ran while one was open for 0% of the time, Pallas kernels for 0%

profile of v1, /device:TPU:1, one launch (start us, length us, event | category | flops | bytes accessed | tf_op | source)
XLA Modules:
  0.0 758.5 jit_solution(12419605949534010153)
XLA Ops:
  7.4 0.0 copy-start
  7.4 0.0 reduce-scatter.3.cloned.1.call-start
  7.4 6.5 stack.2
  13.9 575.4 %all_to_all.10 = bf16[64,12500,8]{1,2,0:T(8,128)(2,1)} all-to-all(bf16[64,12500,8]{1,2,0:T(8,128)(2,1)} %stack.2), channel_id=1, replica_groups=mesh['ia'=64,'jb_0'=4,'jb_1'=2] {'ia'}, dimensions={0} | all-to-all | bytes 25600000 | tf_op jit(solution)/shard_map/all_to_all | solution.py:26
  589.3 0.0 copy-done
  589.3 8.9 %fusion = f32[125,64,8]{0,1,2:T(8,128)} fusion(bf16[64,8,12500]{2,1,0:T(8,128)(2,1)} %bitcast.21, bf16[125,12500]{0,1:T(8,128)(2,1)S(1)} %copy-done), kind=kOutput, calls=%fused_computation | convolution fusion | flops 1600000000 | bytes 16181000 | tf_op jit(solution)/shard_map/dot_general | solution.py:28
  598.2 0.0 reduce-scatter.3.cloned.1.call-update
  598.2 0.0 all-gather.4.cloned.1.call-start
  598.3 0.5 all-gather.4.cloned.1.call-update
  598.8 0.0 reduce-scatter.5.cloned.1.call-start
  598.9 21.5 %reduce-scatter.3.cloned.1.call-done = f32[125,64,2]{0,1,2:T(8,128)} async-done(((f32[125,64,8]{0,1,2:T(8,128)}), f32[125,64,2]{0,1,2:T(8,128)}) %reduce-scatter.3.cloned.1.call-update) | async-done | bytes 64016 | tf_op jit(solution)/shard_map/reduce_scatter | solution.py:17
  620.4 0.0 reduce-scatter.5.cloned.1.call-update
  620.4 98.3 %all-gather.4.cloned.1.call-done = bf16[8,125,1100]{1,2,0:T(8,128)(2,1)} async-done(((bf16[1,125,1100]{1,2,0:T(8,128)(2,1)}), bf16[8,125,1100]{1,2,0:T(8,128)(2,1)}) %all-gather.4.cloned.1.call-update) | async-done | bytes 2200016 | tf_op jit(solution)/shard_map/all_gather | solution.py:12
  718.8 0.0 reduce-scatter.5.cloned.1.call-done
  718.8 1.4 convolution_bitcast_fusion
  720.2 0.3 copy.7
  720.5 29.9 %all_to_all.11 = f32[64,1,1100]{2,1,0:T(1,128)S(1)} all-to-all(f32[64,1,1100]{2,1,0:T(1,128)S(1)} %copy.7), channel_id=1, replica_groups=mesh['ia'=64,'jb_0'=4,'jb_1'=2] {'ia'}, dimensions={0} | all-to-all | bytes 563200 | tf_op jit(solution)/shard_map/all_to_all | solution.py:35
  750.4 0.1 bitcast_reduce_fusion
  750.4 0.6 reduce_sum.12
Async XLA Ops:
  7.4 581.9 %copy-start = (bf16[125,12500]{0,1:T(8,128)(2,1)S(1)}, bf16[125,12500]{0,1:T(8,128)(2,1)}, u32[]{:S(2)}) copy-start(bf16[125,12500]{0,1:T(8,128)(2,1)} %param.3) | copy-start | bytes 9375004
  7.4 613.0 %reduce-scatter.3.cloned.1.call-start = ((), (), s32[]{:S(2)}) async-start(), calls=%async_computation.4 | async-start | bytes 327680 | tf_op jit(solution)/shard_map/reduce_scatter | solution.py:17
  598.2 120.5 %all-gather.4.cloned.1.call-start = ((), (), s32[]{:S(2)}) async-start(), calls=%async_computation.6 | async-start | bytes 2543616 | tf_op jit(solution)/shard_map/all_gather | solution.py:12
  598.8 120.0 %reduce-scatter.5.cloned.1.call-start = ((), (), s32[]{:S(2)}) async-start(), calls=%async_computation.5 | async-start | bytes 98304 | tf_op jit(solution)/shard_map/reduce_scatter | solution.py:17
Sparse Core Ops, SparseCore 0:
  598.4 21.9 reduce-scatter.2
  623.1 33.1 reduce-scatter.4
Sparse Core Ops, SparseCore 1:
  601.9 116.8 all-gather.3
